TPU v7x, 32 devices: a whole 2x2x4 slice. The times are simulated.
32 devices in a mesh: frame: 4 (over x, core), cam: 8 (over z, y).
Axes of the slice: x: 2, y: 2, z: 4, core: 2. Of those that a mesh axis runs over, the one named last changes fastest.
Arguments:
- view_maps: bfloat16 [8, 88, 2, 32, 256], P('frame', 'cam'), may hold values from -6 to 6
- conv_weight: bfloat16 [9, 256, 256], replicated, may hold values from -0.125 to 0.125
- join_weight: bfloat16 [16384, 256], P('cam'), may hold values from -0.1875 to 0.1875
- valid_cams: int32 [8, 88], P('frame'), may hold values from 0 to 1, as said below
- latent_grad: bfloat16 [8, 256], P('frame'), may hold values from -6 to 6
Outputs:
- latent: float32 [8, 256], P('frame')
- conv_grad: float32 [9, 256, 256], replicated
- join_grad: float32 [16384, 256], P(('cam', 'frame'))
Inputs may be any that keep to these rules, and one draw needn't show every extreme that they name: `valid_cams`: every frame has at least one usable camera; the last 6 cameras are padding and never usable.
All inputs are finite; a program needn't handle non-finite values.
Results may differ from a plain program's by a relative error of at most 0.007.
Values may be sent and summed in bfloat16 or wider, within the bound.
A program may use at most 64 MiB of HBM per device.

v0:
```python
import jax
import jax.numpy as jnp
from jax import lax
from jax.sharding import PartitionSpec as P


def make_shifts(maps, rows_n, cols_n, chans):
    padded = jnp.pad(maps, ((0, 0), (0, 0), (1, 1), (1, 1), (0, 0)))
    return [
        padded[:, :, dy : dy + rows_n, dx : dx + cols_n, :].reshape(-1, chans)
        for dy in range(3)
        for dx in range(3)
    ]


def on_device(view_maps, conv_weight, join_weight, valid_cams, latent_grad):
    frames_here, cams_here, rows_n, cols_n, chans = view_maps.shape
    feat_len = rows_n * cols_n * chans
    shifted = make_shifts(view_maps, rows_n, cols_n, chans)
    preact = jnp.zeros((frames_here * cams_here * rows_n * cols_n, chans), jnp.float32)
    for k in range(9):
        preact = preact + jnp.dot(shifted[k], conv_weight[k], preferred_element_type=jnp.float32)
    sigma = jax.nn.sigmoid(preact)
    features = (preact * sigma).astype(jnp.bfloat16)
    features = features.reshape(frames_here, cams_here, feat_len)
    slopes = (sigma * (1.0 + preact * (1.0 - sigma))).reshape(frames_here, cams_here, feat_len)
    cam_count = jnp.sum(valid_cams.astype(jnp.float32), axis=1)
    local_valid = lax.dynamic_slice_in_dim(
        valid_cams, lax.axis_index("cam") * cams_here, cams_here, 1
    )
    mask_f = local_valid.astype(jnp.float32)
    mask_b = local_valid.astype(jnp.bfloat16)
    share_len = feat_len // lax.axis_size("cam")
    pooled = lax.psum_scatter(
        jnp.einsum("fc,fcp->pf", mask_b, features, preferred_element_type=jnp.float32),
        "cam",
        scatter_dimension=0,
        tiled=True,
    )
    joined = (pooled.T / cam_count[:, None]).astype(jnp.bfloat16)
    partial_latent = jnp.dot(joined, join_weight, preferred_element_type=jnp.float32)
    latent = lax.psum(partial_latent, "cam")
    joined_grad = jnp.einsum(
        "fl,sl->fs", latent_grad, join_weight, preferred_element_type=jnp.float32
    ).astype(jnp.bfloat16)
    weighting = mask_f / cam_count[:, None]
    scaled = (
        lax.all_gather(joined_grad, "cam", axis=1, tiled=True).astype(jnp.float32)[:, None, :]
        * weighting[:, :, None]
        * slopes
    )
    pre_grad = scaled.astype(jnp.bfloat16)
    pre_grad = pre_grad.reshape(-1, chans)
    taps = jnp.stack(
        [
            lax.dot_general(
                shifted[k], pre_grad, (((0,), (0,)), ((), ())), preferred_element_type=jnp.float32
            )
            for k in range(9)
        ]
    )
    sub_len = share_len // lax.axis_size("frame")
    all_joined, all_cotangent = (
        lax.all_gather(joined, "frame", axis=0, tiled=True),
        lax.all_gather(latent_grad, "frame", axis=0, tiled=True),
    )
    own_rows = lax.dynamic_slice_in_dim(all_joined, lax.axis_index("frame") * sub_len, sub_len, 1)
    join_grad = lax.dot_general(
        own_rows, all_cotangent, (((0,), (0,)), ((), ())), preferred_element_type=jnp.float32
    )
    conv_grad = lax.psum(taps, ("frame", "cam"))
    return (latent, conv_grad, join_grad)


def solution(mesh):
    in_specs = (
        P("frame", "cam", None, None, None),
        P(),
        P("cam", None),
        P("frame", None),
        P("frame", None),
    )
    out_specs = (P("frame", None), P(), P(("cam", "frame"), None))
    return jax.shard_map(
        on_device, mesh=mesh, in_specs=in_specs, out_specs=out_specs, check_vma=False
    )
```

profile of v0, /device:TPU:0, one launch (start us, length us, event | category | flops | bytes accessed | tf_op | source)
XLA Modules:
  0.0 305.6 jit_solution(8454710060224463295)
XLA Ops:
  8.1 4.9 %pad_slice_fusion = (bf16[2,11,2,32,256]{4,3,2,1,0:T(8,128)(2,1)}, bf16[2,11,2,32,256]{4,3,2,1,0:T(8,128)(2,1)}, bf16[2,11,2,32,256]{4,3,2,1,0:T(8,128)(2,1)}, b...) fusion(bf16[2,11,2,32,256]{4,3,2,1,0:T(8,128)(2,1)} %param.5), kind=kLoop, calls=%fused_computation | loop fusion | bytes 6488064 | tf_op jit(solution)/shard_map/slice | solution.py:10
  13.7 32.4 %all_gather.9 = bf16[2,16384]{1,0:T(2,128)(2,1)S(1)} all-gather(bf16[2,2048]{1,0:T(2,128)(2,1)S(1)} %convolution_convert_fusion), channel_id=1, replica_groups=mesh['frame'=4,'cam'=8] {'cam'}, dimensions={1}, use_global_device_ids=true | all-gather | bytes 73728 | tf_op jit(solution)/shard_map/all_gather | solution.py:48
  46.3 1.4 mul.41
  47.7 1.6 fusion.17
  57.7 1.9 multiply_convert_fusion
  59.6 1.6 reshape.53
  61.6 4.9 %copy.14 = f32[16384,2]{1,0:T(8,128)} copy(f32[16384,2]{0,1:T(2,128)S(1)} %bitcast.140) | data formatting | bytes 262144
  67.6 2.3 fusion.8
  69.9 1.1 fusion.7
  71.0 1.1 fusion.6
  72.2 1.1 fusion.5
  73.3 1.1 fusion.4
  74.4 1.1 fusion.3
  75.5 1.1 fusion.2
  76.6 1.1 fusion.1
  77.7 1.1 fusion
  78.9 5.1 %all-gather.1 = bf16[4,2,256]{2,1,0:T(2,128)(2,1)S(1)} all-gather(bf16[1,2,256]{2,1,0:T(2,128)(2,1)S(1)} %bitcast.141), channel_id=1, replica_groups=mesh['frame'=4,'cam'=8] {'frame'}, dimensions={0}, use_global_device_ids=true | all-gather | bytes 5120 | tf_op jit(solution)/shard_map/all_gather | solution.py:65
  84.0 142.1 %reduce-scatter.4.cloned.1.call-done = f32[2048,2]{1,0:T(8,128)} async-done(((f32[16384,2]{1,0:T(8,128)}), f32[2048,2]{1,0:T(8,128)}) %reduce-scatter.4.cloned.1.call-update) | async-done | bytes 16400
  226.0 1.6 copy.15
  227.7 5.2 %all-gather = bf16[4,2,2048]{2,1,0:T(2,128)(2,1)S(1)} all-gather(bf16[1,2,2048]{2,1,0:T(2,128)(2,1)S(1)} %fusion.68), channel_id=1, replica_groups=mesh['frame'=4,'cam'=8] {'frame'}, dimensions={0}, use_global_device_ids=true | all-gather | bytes 40960 | tf_op jit(solution)/shard_map/all_gather | solution.py:64
  233.2 20.2 %psum.14 = f32[2,256]{1,0:T(2,128)} all-reduce(f32[2,256]{1,0:T(2,128)S(1)} %fusion.34), channel_id=1, replica_groups=mesh['frame'=4,'cam'=8] {'cam'}, use_global_device_ids=true, to_apply=%region_2.3 | all-reduce | flops 512 | bytes 4096 | tf_op jit(solution)/shard_map/psum | solution.py:42
  253.4 1.1 fusion.28
  254.4 40.5 %all-reduce.3.cloned.1.call-done = f32[9,256,256]{2,1,0:T(8,128)} async-done(((f32[9,256,256]{2,1,0:T(8,128)}), f32[9,256,256]{2,1,0:T(8,128)}) %all-reduce.3.cloned.1.call-update) | async-done | bytes 2359312 | tf_op jit(solution)/shard_map/psum | solution.py:71
  294.9 3.2 %copy.29 = f32[9,256,256]{2,1,0:T(8,128)} copy(f32[9,256,256]{2,1,0:T(8,128)} %all-reduce.3.cloned.1.call-done) | data formatting | bytes 4718592
  (65 shorter events, 11.1 us)
Async XLA Ops:
  8.0 5.3 %copy-start = (bf16[2048,256]{1,0:T(8,128)(2,1)S(1)}, bf16[2048,256]{1,0:T(8,128)(2,1)}, u32[]{:S(2)}) copy-start(bf16[2048,256]{1,0:T(8,128)(2,1)} %param.7) | copy-start | bytes 3145732
  8.0 218.0 %reduce-scatter.4.cloned.1.call-start = ((), (), s32[]{:S(2)}) async-start(), calls=%async_computation.2 | async-start | bytes 9437184
  8.1 5.0 %copy-start.20 = (s32[2,88]{1,0:T(2,128)S(1)}, s32[2,88]{1,0:T(2,128)}, u32[]{:S(2)}) copy-start(s32[2,88]{1,0:T(2,128)} %param.8) | copy-start | bytes 2116
  8.1 5.2 %copy-start.19 = (bf16[2,256]{1,0:T(2,128)(2,1)S(1)}, bf16[2,256]{1,0:T(2,128)(2,1)}, u32[]{:S(2)}) copy-start(bf16[2,256]{1,0:T(2,128)(2,1)} %param.9) | copy-start | bytes 3076
  47.7 1.6 copy-start.11
  47.7 1.7 copy-start.15
  49.5 1.1 copy-start.9
  50.6 1.1 copy-start.7
  51.7 1.1 copy-start.1
  52.8 1.1 copy-start.5
  53.9 1.1 copy-start.3
  55.0 1.1 copy-start.2
  56.1 1.4 copy-start.14
  56.1 1.5 copy-start.16
  66.5 1.1 copy-start.13
  66.5 228.4 %all-reduce.3.cloned.1.call-start = ((), (), s32[]{:S(2)}) async-start(), calls=%async_computation.1 | async-start | bytes 4718592 | tf_op jit(solution)/shard_map/psum | solution.py:71
  66.6 3.3 %copy-start.12 = (bf16[2,11,2,32,256]{4,3,2,1,0:T(8,128)(2,1)S(1)}, bf16[2,11,2,32,256]{4,3,2,1,0:T(8,128)(2,1)}, u32[]{:S(2)}) copy-start(bf16[2,11,2,32,256]{4,3,2,1,0:T(8,128)(2,1)} %get-tuple-element.6) | copy-start | bytes 2162692
  66.6 3.3 %copy-start.18 = (bf16[1408,256]{1,0:T(8,128)(2,1)S(1)}, bf16[1408,256]{1,0:T(8,128)(2,1)}, u32[]{:S(2)}) copy-start(bf16[1408,256]{1,0:T(8,128)(2,1)} %get-tuple-element.3) | copy-start | bytes 2162692
  67.6 3.4 %copy-start.10 = (bf16[2,11,2,32,256]{4,3,2,1,0:T(8,128)(2,1)S(1)}, bf16[2,11,2,32,256]{4,3,2,1,0:T(8,128)(2,1)}, u32[]{:S(2)}) copy-start(bf16[2,11,2,32,256]{4,3,2,1,0:T(8,128)(2,1)} %get-tuple-element.7) | copy-start | bytes 2162692
  69.9 2.2 copy-start.8
  72.2 2.2 copy-start.6
  73.3 2.2 copy-start.4
  75.5 2.2 copy-start.17
Sparse Core Ops, SparseCore 0:
  66.7 159.3 reduce-scatter.3
Sparse Core Ops, SparseCore 1:
  79.0 215.9 all-reduce.2
where the time goes:
time: 306 us
  waiting for transfers between devices  183 us (60%)
  blocking collectives  62.8 us (21%)
  local copies, waits for them, and re-layouts  24.7 us (8%)
  matrix products  19.2 us (6%)
  between operations  15.6 us (5%)
    unnamed x3, waiting for transfers between devices  142 us
    psum x1, waiting for transfers between devices, on_device(): conv_grad = lax.psum(taps, ('frame', 'cam'))  40.5 us
    all_gather x1, blocking collectives, on_device(): lax.all_gather(joined_grad, 'cam', axis=1, tiled=True).astype(jnp.float32)  32.4 us
    psum x1, blocking collectives, on_device(): latent = lax.psum(partial_latent, 'cam')  20.2 us
    unnamed x47, local copies, waits for them, and re-layouts  16.6 us
    dot_general x9, matrix products, on_device(): lax.dot_general(shifted[k], pre_grad, (((0,), (0,)), ((), ())), preferred...  11.2 us
  transfers between devices with their start and end apart: 2, of which 2 were waited for; matrix products, arithmetic and copies ran while one was open for 5% of the time, Pallas kernels for 0%

commit v1 on v0

--- a/solution.py
+++ b/solution.py
@@ -44,8 +44,28 @@
         "fl,sl->fs", latent_grad, join_weight, preferred_element_type=jnp.float32
     ).astype(jnp.bfloat16)
     weighting = mask_f / cam_count[:, None]
+
+    def time_things_all(field_in):
+        mixed_arr = lax.axis_size("cam")
+        answer, outcome_arr, o_now = (mixed_arr, lax.axis_index("cam"), field_in.shape[1])
+        finding, v_now = (field_in, 1)
+        while v_now < answer:
+            finding = jnp.concatenate(
+                [
+                    finding,
+                    lax.ppermute(
+                        finding,
+                        axis_name="cam",
+                        perm=list(map(lambda i0: (i0, (i0 - v_now) % answer), range(answer))),
+                    ),
+                ],
+                1,
+            )
+            v_now = 2 * v_now
+        return jnp.roll(finding, outcome_arr * o_now, 1)
+
     scaled = (
-        lax.all_gather(joined_grad, "cam", axis=1, tiled=True).astype(jnp.float32)[:, None, :]
+        time_things_all(joined_grad).astype(jnp.float32)[:, None, :]
         * weighting[:, :, None]
         * slopes
     )

time: 306 us -> 292 us (0.954)
  blocking collectives: 62.8 us -> 30.4 us
  waiting for transfers between devices: 183 us -> 198 us
  starting transfers between devices: 0.08 us -> 6.67 us
  matrix products: 19.2 us -> 13 us
  other arithmetic: 0.61 us -> 3.8 us
    all_gather x1 -> x0, blocking collectives: 32.4 us -> none  [on_device(): lax.all_gather(joined_grad, 'cam', axis=1, tiled=True).astype(jnp.float32)]
    ppermute x0 -> x3, waiting for transfers between devices: none -> 8.07 us  [time_things_all(): lax.ppermute(finding, axis_name='cam', perm=list(map(lambda i0: (i0, (i0...]
    unnamed x3, waiting for transfers between devices: 142 us -> 150 us
    dot_general x9, matrix products: 11.2 us -> 4.42 us  [on_device(): lax.dot_general(shifted[k], pre_grad, (((0,), (0,)), ((), ())), preferred...]
    ppermute x0 -> x3, starting transfers between devices: none -> 6.59 us  [time_things_all(): lax.ppermute(finding, axis_name='cam', perm=list(map(lambda i0: (i0, (i0...]
    unnamed x47 -> x55, local copies, waits for them, and re-layouts: 16.6 us -> 18.9 us
  transfers between devices with their start and end apart: 2 -> 5, of which waited for: 2 -> 4; matrix products, arithmetic and copies ran while one was open for 5% -> 5% of each run, Pallas kernels for 0% -> 0%
where the time goes in v1:
time: 292 us; the launch traced here: 291 us
  waiting for transfers between devices  198 us (68%)
  blocking collectives  30.4 us (10%)
  local copies, waits for them, and re-layouts  23.4 us (8%)
  between operations  15.8 us (5%)
  matrix products  13 us (4%)
  starting transfers between devices  6.67 us (2%)
  other arithmetic  3.8 us (1%)
    unnamed x3, waiting for transfers between devices  150 us
    psum x1, waiting for transfers between devices, on_device(): conv_grad = lax.psum(taps, ('frame', 'cam'))  40.5 us
    psum x1, blocking collectives, on_device(): latent = lax.psum(partial_latent, 'cam')  20.2 us
    unnamed x55, local copies, waits for them, and re-layouts  18.9 us
    ppermute x3, waiting for transfers between devices, time_things_all(): lax.ppermute(finding, axis_name='cam', perm=list(map(lambda i0: (i0, (i0...  8.07 us
    ppermute x3, starting transfers between devices, time_things_all(): lax.ppermute(finding, axis_name='cam', perm=list(map(lambda i0: (i0, (i0...  6.59 us
    dot_general x9, matrix products, on_device(): jnp.dot(shifted[k], conv_weight[k], preferred_element_type=jnp.float32)  5.93 us
  transfers between devices with their start and end apart: 5, of which 4 were waited for; matrix products, arithmetic and copies ran while one was open for 5% of the time, Pallas kernels for 0%

profile of v1, /device:TPU:0, one launch (start us, length us, event | category | flops | bytes accessed | tf_op | source)
XLA Modules:
  0.0 291.4 jit_solution(17301035568372068742)
XLA Ops:
  8.1 1.2 copy-done
  9.2 1.0 constant_dynamic-update-slice_fusion.7
  10.3 6.0 %collective-permute-start = (bf16[2,2048]{1,0:T(2,128)(2,1)S(1)}, bf16[2,2048]{1,0:T(2,128)(2,1)S(1)}, u32[]{:S(2)}, u32[]{:S(2)}) collective-permute-start(bf16[2,2048]{1,0:T(2,128)(2,1)S(1)} %get-tuple-element.14), channel_id=1, source_target_pairs={{0,7},{1,0},{2,1},{3,2},{4,3},{5,4},{6,5},{7,6},{8,15},{9,8},{10,9... | collective-permute-start | bytes 24584 | tf_op jit(solution)/shard_map/ppermute | solution.py:56
  16.3 0.8 convert_reduce_fusion
  17.1 2.5 pad_slice_fusion
  19.7 2.0 fusion.17
  23.3 0.8 copy-done.11
  27.4 1.5 convolution_add_fusion
  29.5 3.3 %collective-permute-done.1 = bf16[2,4096]{1,0:T(2,128)(2,1)S(1)} collective-permute-done((bf16[2,4096]{1,0:T(2,128)(2,1)S(1)}, bf16[2,4096]{1,0:T(2,128)(2,1)S(1)}, u32[]{:S(2)}, u32[]{:S(2)}) %collective-permute-start.1) | collective-permute-done | bytes 16416 | tf_op jit(solution)/shard_map/ppermute | solution.py:56
  32.9 4.8 %collective-permute-done.2 = bf16[2,8192]{1,0:T(2,128)(2,1)S(1)} collective-permute-done((bf16[2,8192]{1,0:T(2,128)(2,1)S(1)}, bf16[2,8192]{1,0:T(2,128)(2,1)S(1)}, u32[]{:S(2)}, u32[]{:S(2)}) %collective-permute-start.2) | collective-permute-done | bytes 32800 | tf_op jit(solution)/shard_map/ppermute | solution.py:56
  38.1 1.4 mul.45
  39.5 2.5 multiply_convert_fusion
  47.0 1.4 copy-done.18
  49.3 5.0 %copy.14 = f32[16384,2]{1,0:T(8,128)} copy(f32[16384,2]{0,1:T(2,128)S(1)} %bitcast.138) | data formatting | bytes 262144
  54.3 1.0 copy-done.4
  55.4 1.1 fusion
  57.1 5.1 %all-gather.1 = bf16[4,2,256]{2,1,0:T(2,128)(2,1)S(1)} all-gather(bf16[1,2,256]{2,1,0:T(2,128)(2,1)S(1)} %bitcast.139), channel_id=1, replica_groups=mesh['frame'=4,'cam'=8] {'frame'}, dimensions={0}, use_global_device_ids=true | all-gather | bytes 5120 | tf_op jit(solution)/shard_map/all_gather | solution.py:85
  62.2 149.6 %reduce-scatter.4.cloned.1.call-done = f32[2048,2]{1,0:T(8,128)} async-done(((f32[16384,2]{1,0:T(8,128)}), f32[2048,2]{1,0:T(8,128)}) %reduce-scatter.4.cloned.1.call-update) | async-done | bytes 16400
  211.8 1.6 copy.15
  213.5 5.2 %all-gather = bf16[4,2,2048]{2,1,0:T(2,128)(2,1)S(1)} all-gather(bf16[1,2,2048]{2,1,0:T(2,128)(2,1)S(1)} %fusion.69), channel_id=1, replica_groups=mesh['frame'=4,'cam'=8] {'frame'}, dimensions={0}, use_global_device_ids=true | all-gather | bytes 40960 | tf_op jit(solution)/shard_map/all_gather | solution.py:84
  219.0 20.2 %psum.14 = f32[2,256]{1,0:T(2,128)} all-reduce(f32[2,256]{1,0:T(2,128)S(1)} %fusion.35), channel_id=1, replica_groups=mesh['frame'=4,'cam'=8] {'cam'}, use_global_device_ids=true, to_apply=%region_2.3 | all-reduce | flops 512 | bytes 4096 | tf_op jit(solution)/shard_map/psum | solution.py:42
  239.2 1.1 fusion.28
  240.3 40.5 %all-reduce.3.cloned.1.call-done = f32[9,256,256]{2,1,0:T(8,128)} async-done(((f32[9,256,256]{2,1,0:T(8,128)}), f32[9,256,256]{2,1,0:T(8,128)}) %all-reduce.3.cloned.1.call-update) | async-done | bytes 2359312 | tf_op jit(solution)/shard_map/psum | solution.py:91
  280.7 3.2 %copy.36 = f32[9,256,256]{2,1,0:T(8,128)} copy(f32[9,256,256]{2,1,0:T(8,128)} %all-reduce.3.cloned.1.call-done) | data formatting | bytes 4718592
  (82 shorter events, 12.9 us)
Async XLA Ops:
  8.0 1.2 copy-start
  8.0 9.1 %copy-start.1 = (bf16[2,11,2,32,256]{4,3,2,1,0:T(8,128)(2,1)S(1)}, bf16[2,11,2,32,256]{4,3,2,1,0:T(8,128)(2,1)}, u32[]{:S(2)}) copy-start(bf16[2,11,2,32,256]{4,3,2,1,0:T(8,128)(2,1)} %param.5) | copy-start | bytes 2162692
  8.0 203.8 %reduce-scatter.4.cloned.1.call-start = ((), (), s32[]{:S(2)}) async-start(), calls=%async_computation.2 | async-start | bytes 9437184
  10.3 18.7 %collective-permute-start = (bf16[2,2048]{1,0:T(2,128)(2,1)S(1)}, bf16[2,2048]{1,0:T(2,128)(2,1)S(1)}, u32[]{:S(2)}, u32[]{:S(2)}) collective-permute-start(bf16[2,2048]{1,0:T(2,128)(2,1)S(1)} %get-tuple-element.14), channel_id=1, source_target_pairs={{0,7},{1,0},{2,1},{3,2},{4,3},{5,4},{6,5},{7,6},{8,15},{9,8},{10,9... | collective-permute-start | bytes 24584 | tf_op jit(solution)/shard_map/ppermute | solution.py:56
  17.1 2.5 copy-start.21
  19.6 7.4 %copy-start.5 = (bf16[2,11,2,32,256]{4,3,2,1,0:T(8,128)(2,1)}, bf16[2,11,2,32,256]{4,3,2,1,0:T(8,128)(2,1)S(1)}, u32[]{:S(2)}) copy-start(bf16[2,11,2,32,256]{4,3,2,1,0:T(8,128)(2,1)S(1)} %get-tuple-element.11) | copy-start | bytes 2162692
  19.6 7.8 %copy-start.3 = (bf16[2,11,2,32,256]{4,3,2,1,0:T(8,128)(2,1)}, bf16[2,11,2,32,256]{4,3,2,1,0:T(8,128)(2,1)S(1)}, u32[]{:S(2)}) copy-start(bf16[2,11,2,32,256]{4,3,2,1,0:T(8,128)(2,1)S(1)} %get-tuple-element.5) | copy-start | bytes 2162692
  19.6 2.1 copy-start.15
  19.6 2.3 copy-start.19
  21.9 1.1 copy-start.13
  23.0 1.1 copy-start.11
  24.4 1.1 copy-start.9
  29.0 3.8 %collective-permute-start.1 = (bf16[2,4096]{1,0:T(2,128)(2,1)S(1)}, bf16[2,4096]{1,0:T(2,128)(2,1)S(1)}, u32[]{:S(2)}, u32[]{:S(2)}) collective-permute-start(bf16[2,4096]{1,0:T(2,128)(2,1)S(1)} %pad_maximum_fusion.1), channel_id=1, source_target_pairs={{0,6},{1,7},{2,0},{3,1},{4,2},{5,3},{6,4},{7,5},{8,14},{9,15},{10,... | collective-permute-start | bytes 49160 | tf_op jit(solution)/shard_map/ppermute | solution.py:56
  32.8 4.9 %collective-permute-start.2 = (bf16[2,8192]{1,0:T(2,128)(2,1)S(1)}, bf16[2,8192]{1,0:T(2,128)(2,1)S(1)}, u32[]{:S(2)}, u32[]{:S(2)}) collective-permute-start(bf16[2,8192]{1,0:T(2,128)(2,1)S(1)} %pad_maximum_fusion), channel_id=1, source_target_pairs={{0,4},{1,5},{2,6},{3,7},{4,0},{5,1},{6,2},{7,3},{8,12},{9,13},{10,... | collective-permute-start | bytes 98312 | tf_op jit(solution)/shard_map/ppermute | solution.py:56
  39.5 2.5 copy-start.17
  42.0 1.1 copy-start.16
  42.0 1.5 copy-start.14
  43.1 1.2 copy-start.12
  43.5 1.2 copy-start.2
  44.3 1.2 copy-start.10
  44.7 1.2 copy-start.8
  45.4 1.2 copy-start.6
  47.0 1.4 copy-start.18
  54.3 226.5 %all-reduce.3.cloned.1.call-start = ((), (), s32[]{:S(2)}) async-start(), calls=%async_computation.1 | async-start | bytes 4718592 | tf_op jit(solution)/shard_map/psum | solution.py:91
  (3 other events, 2.9 us)
Sparse Core Ops, SparseCore 0:
  54.4 157.3 reduce-scatter.3
Sparse Core Ops, SparseCore 1:
  60.9 219.8 all-reduce.2
